TPU v7x, 256 devices: a whole 4x4x8 slice. The times are simulated.
256 devices in a mesh: row: 32 (over x_hi, z, core), col: 8 (over y, x_lo).
Axes of the slice: x: 4 (x_hi: 2, x_lo: 2; x = x_hi * 2 + x_lo), y: 4, z: 8, core: 2. Of those that a mesh axis runs over, the one named last changes fastest.
Arguments:
- p_tiles: bfloat16 [1024, 2, 128, 128], P(('row', 'col')), may hold values from -0.5 to 0.5
- p_cols: int32 [1024, 2], P(('row', 'col')), may hold values from 0 to 31, as said below
- q_tiles: bfloat16 [1024, 6, 128, 128], P(('row', 'col')), may hold values from -1.796875 to 1.796875
- q_cols: int32 [1024, 6], P(('row', 'col')), may hold values from 0 to 31, all different within a row
Outputs:
- coarse: float32 [4096, 4096], P('row', 'col')
Inputs may be any that keep to these rules, and one draw needn't show every extreme that they name: `p_cols`: the 2 coarse tiles in one row differ; among the fine blocks held by the devices of one index of col, every coarse tile is named at least once and at most 16 times, and some tile exactly 16 times. `q_cols`: the 6 coarse tiles in one row differ; every coarse tile appears somewhere.
All inputs are finite; a program needn't handle non-finite values.
Results may differ from a plain program's by a relative error of at most 0.0003.
Values may be sent and summed in bfloat16 or wider, within the bound.
A program may use at most 128 MiB of HBM per device.

v0:
```python
import math
import jax
import jax.numpy as jnp
from jax import lax
from jax.sharding import PartitionSpec as P


def spread_tiles(tile_set, columns, tile_count):
    blocks, per_block, extent, _ = tile_set.shape
    flipped = jnp.swapaxes(tile_set, 2, 3)
    fine_ids = jnp.broadcast_to(jnp.arange(blocks, dtype=jnp.int32)[:, None], (blocks, per_block))
    placed = jnp.zeros((tile_count, extent, blocks, extent), tile_set.dtype)
    placed = placed.at[columns, :, fine_ids, :].set(flipped)
    return placed.reshape(tile_count * extent, blocks * extent)


def fold_tiles(summed, transposed, tile_set, columns):
    blocks, per_block, extent, _ = tile_set.shape
    height = transposed.shape[0]
    bundle = math.gcd(blocks, 8)
    tile_groups = tile_set.reshape(blocks // bundle, bundle, per_block, extent, extent)
    column_groups = columns.reshape(blocks // bundle, bundle * per_block)

    def one_group(running, inputs):
        position, bundle_tiles, coarse_ids = inputs
        offset = position * bundle * extent
        stripe = lax.dynamic_slice_in_dim(transposed, offset, bundle * extent, 1).reshape(
            height, bundle, extent
        )
        product = jnp.einsum(
            "rfa,fkab->rfkb", stripe, bundle_tiles, preferred_element_type=jnp.float32
        )
        tiled = running.reshape(height, -1, extent)
        tiled = tiled.at[:, coarse_ids, :].add(product.reshape(height, bundle * per_block, extent))
        return (tiled.reshape(height, -1), None)

    counter = jnp.arange(blocks // bundle, dtype=jnp.int32)
    summed, _ = lax.scan(one_group, summed, (counter, tile_groups, column_groups))
    return summed


def body(p_tiles, p_cols, q_tiles, q_cols):
    extent = p_tiles.shape[2]
    tile_count = lax.axis_size("row")
    expanded = spread_tiles(p_tiles, p_cols, tile_count)
    transposed = lax.all_to_all(expanded, "row", split_axis=0, concat_axis=1, tiled=True)
    empty = jnp.zeros((transposed.shape[0], tile_count * extent), jnp.float32)
    partial_sum = fold_tiles(
        empty,
        transposed,
        lax.all_gather(q_tiles, "row", axis=0, tiled=True),
        lax.all_gather(q_cols, "row", axis=0, tiled=True),
    )
    return lax.psum_scatter(partial_sum, "col", scatter_dimension=1, tiled=True)


def solution(mesh):
    placed = (
        P(("row", "col"), None, None, None),
        P(("row", "col"), None),
        P(("row", "col"), None, None, None),
        P(("row", "col"), None),
    )
    return jax.shard_map(
        body, mesh=mesh, in_specs=placed, out_specs=P("row", "col"), check_vma=False
    )
```

profile of v0, /device:TPU:1, one launch (start us, length us, event | category | flops | bytes accessed | tf_op | source)
XLA Modules:
  0.0 604.4 jit_solution(11690526982969184347)
XLA Ops:
  9.3 3.0 broadcast_in_dim.18
  12.3 2.3 scatter_fusion.1
  14.5 6.5 %copy.24 = bf16[32,128,4,128]{1,3,2,0:T(8,128)(2,1)} copy(bf16[32,128,4,128]{3,1,2,0:T(8,128)(2,1)} %scatter_fusion.1) | data formatting | bytes 8388608 | tf_op jit(solution)/shard_map/scatter | solution.py:13
  21.0 12.8 %all-to-all-start = ((bf16[32,128,512]{1,2,0:T(8,128)(2,1)}), bf16[32,128,512]{1,2,0:T(8,128)(2,1)}, u32[]{:S(2)}, u32[]{:S(2)}) async-start(bf16[32,128,512]{1,2,0:T(8,128)(2,1)} %bitcast.65), calls=%async_computation | async-start | bytes 8388608 | tf_op jit(solution)/shard_map/all_to_all | solution.py:46
  33.8 154.7 %all-gather = s32[32,4,6]{2,1,0:T(4,128)S(1)} all-gather(s32[1,4,6]{2,1,0:T(4,128)S(1)} %bitcast.68), channel_id=1, replica_groups=mesh['row'=32,'col'=8] {'row'}, dimensions={0}, use_global_device_ids=true | all-gather | bytes 3168 | tf_op jit(solution)/shard_map/all_gather | solution.py:52
  188.6 77.6 %all-gather.3.cloned.1.call-done = bf16[128,6,128,128]{3,2,1,0:T(8,128)(2,1)} async-done(((bf16[4,6,128,128]{3,2,1,0:T(8,128)(2,1)}), bf16[128,6,128,128]{3,2,1,0:T(8,128)(2,1)}) %all-gather.3.cloned.1.call-update) | async-done | bytes 25165840 | tf_op jit(solution)/shard_map/all_gather | solution.py:51
  267.7 274.9 %while.12 = (s32[]{:T(128)}, f32[128,4096]{0,1:T(8,128)}, s32[16,48]{1,0:T(8,128)S(1)}, bf16[16,8,6,128,128]{4,3,2,1,0:T(8,128)(2,1)}, s32[16]{0:T(128)S(1)}, /*...) while((s32[]{:T(128)}, f32[128,4096]{0,1:T(8,128)}, ...), condition=%wide.region_3.4_spmd, body=%wide.region_1.3_spmd.sunk | while | flops 202113168 | bytes 29623528 | solution.py:38
  269.9 2.1 fusion.17
  272.0 2.4 copy.35
  276.3 6.7 %scatter_fusion = f32[128,32,128]{2,0,1:T(8,128)S(1)} fusion(f32[128,32,128]{2,0,1:T(8,128)S(1)} %copy.34, s32[48]{0:T(128)S(1)} %fusion.16, f32[48,128,128]{2,1,0:T(8,128)} %bitcast.61), kind=kCustom, calls=%fused_computation.clone.1 | custom fusion | flops 786432 | bytes 9437376 | tf_op jit(solution)/shard_map/while/body/eval_jaxpr/scatter-add | solution.py:34
  289.2 2.4 copy.35
  293.5 6.7 %scatter_fusion = f32[128,32,128]{2,0,1:T(8,128)S(1)} fusion(f32[128,32,128]{2,0,1:T(8,128)S(1)} %copy.34, s32[48]{0:T(128)S(1)} %fusion.16, f32[48,128,128]{2,1,0:T(8,128)} %bitcast.61), kind=kCustom, calls=%fused_computation.clone.1 | custom fusion | flops 786432 | bytes 9437376 | tf_op jit(solution)/shard_map/while/body/eval_jaxpr/scatter-add | solution.py:34
  304.3 2.1 fusion.17
  306.4 2.4 copy.35
  310.7 6.7 %scatter_fusion = f32[128,32,128]{2,0,1:T(8,128)S(1)} fusion(f32[128,32,128]{2,0,1:T(8,128)S(1)} %copy.34, s32[48]{0:T(128)S(1)} %fusion.16, f32[48,128,128]{2,1,0:T(8,128)} %bitcast.61), kind=kCustom, calls=%fused_computation.clone.1 | custom fusion | flops 786432 | bytes 9437376 | tf_op jit(solution)/shard_map/while/body/eval_jaxpr/scatter-add | solution.py:34
  323.5 2.4 copy.35
  327.8 6.7 %scatter_fusion = f32[128,32,128]{2,0,1:T(8,128)S(1)} fusion(f32[128,32,128]{2,0,1:T(8,128)S(1)} %copy.34, s32[48]{0:T(128)S(1)} %fusion.16, f32[48,128,128]{2,1,0:T(8,128)} %bitcast.61), kind=kCustom, calls=%fused_computation.clone.1 | custom fusion | flops 786432 | bytes 9437376 | tf_op jit(solution)/shard_map/while/body/eval_jaxpr/scatter-add | solution.py:34
  340.7 2.4 copy.35
  345.0 6.7 %scatter_fusion = f32[128,32,128]{2,0,1:T(8,128)S(1)} fusion(f32[128,32,128]{2,0,1:T(8,128)S(1)} %copy.34, s32[48]{0:T(128)S(1)} %fusion.16, f32[48,128,128]{2,1,0:T(8,128)} %bitcast.61), kind=kCustom, calls=%fused_computation.clone.1 | custom fusion | flops 786432 | bytes 9437376 | tf_op jit(solution)/shard_map/while/body/eval_jaxpr/scatter-add | solution.py:34
  357.9 2.4 copy.35
  362.2 6.7 %scatter_fusion = f32[128,32,128]{2,0,1:T(8,128)S(1)} fusion(f32[128,32,128]{2,0,1:T(8,128)S(1)} %copy.34, s32[48]{0:T(128)S(1)} %fusion.16, f32[48,128,128]{2,1,0:T(8,128)} %bitcast.61), kind=kCustom, calls=%fused_computation.clone.1 | custom fusion | flops 786432 | bytes 9437376 | tf_op jit(solution)/shard_map/while/body/eval_jaxpr/scatter-add | solution.py:34
  373.0 2.1 fusion.17
  375.1 2.4 copy.35
  379.4 6.7 %scatter_fusion = f32[128,32,128]{2,0,1:T(8,128)S(1)} fusion(f32[128,32,128]{2,0,1:T(8,128)S(1)} %copy.34, s32[48]{0:T(128)S(1)} %fusion.16, f32[48,128,128]{2,1,0:T(8,128)} %bitcast.61), kind=kCustom, calls=%fused_computation.clone.1 | custom fusion | flops 786432 | bytes 9437376 | tf_op jit(solution)/shard_map/while/body/eval_jaxpr/scatter-add | solution.py:34
  392.3 2.4 copy.35
  396.6 6.7 %scatter_fusion = f32[128,32,128]{2,0,1:T(8,128)S(1)} fusion(f32[128,32,128]{2,0,1:T(8,128)S(1)} %copy.34, s32[48]{0:T(128)S(1)} %fusion.16, f32[48,128,128]{2,1,0:T(8,128)} %bitcast.61), kind=kCustom, calls=%fused_computation.clone.1 | custom fusion | flops 786432 | bytes 9437376 | tf_op jit(solution)/shard_map/while/body/eval_jaxpr/scatter-add | solution.py:34
  409.4 2.4 copy.35
  413.7 6.7 %scatter_fusion = f32[128,32,128]{2,0,1:T(8,128)S(1)} fusion(f32[128,32,128]{2,0,1:T(8,128)S(1)} %copy.34, s32[48]{0:T(128)S(1)} %fusion.16, f32[48,128,128]{2,1,0:T(8,128)} %bitcast.61), kind=kCustom, calls=%fused_computation.clone.1 | custom fusion | flops 786432 | bytes 9437376 | tf_op jit(solution)/shard_map/while/body/eval_jaxpr/scatter-add | solution.py:34
  424.6 2.1 fusion.17
  426.6 2.4 copy.35
  430.9 6.7 %scatter_fusion = f32[128,32,128]{2,0,1:T(8,128)S(1)} fusion(f32[128,32,128]{2,0,1:T(8,128)S(1)} %copy.34, s32[48]{0:T(128)S(1)} %fusion.16, f32[48,128,128]{2,1,0:T(8,128)} %bitcast.61), kind=kCustom, calls=%fused_computation.clone.1 | custom fusion | flops 786432 | bytes 9437376 | tf_op jit(solution)/shard_map/while/body/eval_jaxpr/scatter-add | solution.py:34
  443.8 2.4 copy.35
  448.1 6.7 %scatter_fusion = f32[128,32,128]{2,0,1:T(8,128)S(1)} fusion(f32[128,32,128]{2,0,1:T(8,128)S(1)} %copy.34, s32[48]{0:T(128)S(1)} %fusion.16, f32[48,128,128]{2,1,0:T(8,128)} %bitcast.61), kind=kCustom, calls=%fused_computation.clone.1 | custom fusion | flops 786432 | bytes 9437376 | tf_op jit(solution)/shard_map/while/body/eval_jaxpr/scatter-add | solution.py:34
  461.0 2.4 copy.35
  465.3 6.7 %scatter_fusion = f32[128,32,128]{2,0,1:T(8,128)S(1)} fusion(f32[128,32,128]{2,0,1:T(8,128)S(1)} %copy.34, s32[48]{0:T(128)S(1)} %fusion.16, f32[48,128,128]{2,1,0:T(8,128)} %bitcast.61), kind=kCustom, calls=%fused_computation.clone.1 | custom fusion | flops 786432 | bytes 9437376 | tf_op jit(solution)/shard_map/while/body/eval_jaxpr/scatter-add | solution.py:34
  476.1 2.1 fusion.17
  478.2 2.4 copy.35
  482.5 6.7 %scatter_fusion = f32[128,32,128]{2,0,1:T(8,128)S(1)} fusion(f32[128,32,128]{2,0,1:T(8,128)S(1)} %copy.34, s32[48]{0:T(128)S(1)} %fusion.16, f32[48,128,128]{2,1,0:T(8,128)} %bitcast.61), kind=kCustom, calls=%fused_computation.clone.1 | custom fusion | flops 786432 | bytes 9437376 | tf_op jit(solution)/shard_map/while/body/eval_jaxpr/scatter-add | solution.py:34
  493.3 2.1 fusion.17
  495.3 2.4 copy.35
  499.6 6.7 %scatter_fusion = f32[128,32,128]{2,0,1:T(8,128)S(1)} fusion(f32[128,32,128]{2,0,1:T(8,128)S(1)} %copy.34, s32[48]{0:T(128)S(1)} %fusion.16, f32[48,128,128]{2,1,0:T(8,128)} %bitcast.61), kind=kCustom, calls=%fused_computation.clone.1 | custom fusion | flops 786432 | bytes 9437376 | tf_op jit(solution)/shard_map/while/body/eval_jaxpr/scatter-add | solution.py:34
  510.5 2.1 fusion.17
  512.5 2.4 copy.35
  516.8 6.7 %scatter_fusion = f32[128,32,128]{2,0,1:T(8,128)S(1)} fusion(f32[128,32,128]{2,0,1:T(8,128)S(1)} %copy.34, s32[48]{0:T(128)S(1)} %fusion.16, f32[48,128,128]{2,1,0:T(8,128)} %bitcast.61), kind=kCustom, calls=%fused_computation.clone.1 | custom fusion | flops 786432 | bytes 9437376 | tf_op jit(solution)/shard_map/while/body/eval_jaxpr/scatter-add | solution.py:34
  529.7 2.4 copy.35
  534.0 6.7 %scatter_fusion = f32[128,32,128]{2,0,1:T(8,128)S(1)} fusion(f32[128,32,128]{2,0,1:T(8,128)S(1)} %copy.34, s32[48]{0:T(128)S(1)} %fusion.16, f32[48,128,128]{2,1,0:T(8,128)} %bitcast.61), kind=kCustom, calls=%fused_computation.clone.1 | custom fusion | flops 786432 | bytes 9437376 | tf_op jit(solution)/shard_map/while/body/eval_jaxpr/scatter-add | solution.py:34
  542.6 2.9 copy.26
  545.5 52.1 %reduce-scatter.2.cloned.1.call-done = f32[128,512]{1,0:T(8,128)} async-done(((f32[128,4096]{1,0:T(8,128)}), f32[128,512]{1,0:T(8,128)}) %reduce-scatter.2.cloned.1.call-update) | async-done | bytes 262160 | tf_op jit(solution)/shard_map/reduce_scatter | solution.py:54
  (103 shorter events, 108.7 us)
Async XLA Ops:
  6.5 259.7 %all-gather.3.cloned.1.call-start = ((), (), s32[]{:S(2)}) async-start(), calls=%async_computation.2 | async-start | bytes 25952256 | tf_op jit(solution)/shard_map/all_gather | solution.py:51
  21.0 12.8 %copy-start = (s32[4,6]{1,0:T(4,128)S(1)}, s32[4,6]{1,0:T(4,128)}, u32[]{:S(2)}) copy-start(s32[4,6]{1,0:T(4,128)} %param.9) | copy-start | bytes 292
  21.0 167.6 %all-to-all-start = ((bf16[32,128,512]{1,2,0:T(8,128)(2,1)}), bf16[32,128,512]{1,2,0:T(8,128)(2,1)}, u32[]{:S(2)}, u32[]{:S(2)}) async-start(bf16[32,128,512]{1,2,0:T(8,128)(2,1)} %bitcast.65), calls=%async_computation | async-start | bytes 8388608 | tf_op jit(solution)/shard_map/all_to_all | solution.py:46
  33.8 563.8 %reduce-scatter.2.cloned.1.call-start = ((), (), s32[]{:S(2)}) async-start(), calls=%async_computation.3 | async-start | bytes 2359296 | tf_op jit(solution)/shard_map/reduce_scatter | solution.py:54
Sparse Core Ops, SparseCore 0:
  10.1 256.0 all-gather.2
  545.6 51.9 reduce-scatter.1
where the time goes:
time: 608 us; the launch traced here: 604 us
  blocking collectives  155 us (25%)
  local copies, waits for them, and re-layouts  141 us (23%)
  waiting for transfers between devices  130 us (21%)
  other arithmetic  109 us (18%)
  matrix products  33 us (5%)
  between operations  13.4 us (2%)
  starting transfers between devices  12.8 us (2%)
  loops' own time  10.5 us (2%)
    all_gather x1, blocking collectives, body(): lax.all_gather(q_cols, 'row', axis=0, tiled=True)  155 us
    scatter-add x16, other arithmetic, one_group(): tiled.at[:, coarse_ids, :]  108 us
    all_gather x1, waiting for transfers between devices, body(): lax.all_gather(q_tiles, 'row', axis=0, tiled=True)  77.6 us
    reduce_scatter x1, waiting for transfers between devices, body(): return lax.psum_scatter(partial_sum, 'col', scatter_dimension=1, tiled=True)  52.1 us
    reshape x16, local copies, waits for them, and re-layouts, one_group(): product.reshape(height, bundle * per_block, extent)  37.8 us
    dot_general x16, matrix products, one_group(): jnp.einsum('rfa,fkab->rfkb', stripe, bundle_tiles, preferred_element_type...  33 us
    reshape x16, local copies, waits for them, and re-layouts, one_group(): tiled = running.reshape(height, -1, extent)  30.7 us
    scatter-add x16, local copies, waits for them, and re-layouts, one_group(): tiled.at[:, coarse_ids, :]  29.2 us
  transfers between devices with their start and end apart: 3, of which 2 were waited for; matrix products, arithmetic and copies ran while one was open for 2% of the time, Pallas kernels for 0%

commit v1 on v0

--- a/solution.py
+++ b/solution.py
@@ -3,6 +3,19 @@
 import jax.numpy as jnp
 from jax import lax
 from jax.sharding import PartitionSpec as P
+
+
+def _apply_task(xin, in_dim, d0):
+    piece_now = jnp.concatenate(
+        lax.all_to_all(
+            jnp.stack(jnp.split(xin, lax.axis_size("row"), axis=in_dim)),
+            axis_name="row",
+            split_axis=0,
+            concat_axis=0,
+        ),
+        axis=d0,
+    )
+    return piece_now
 
 
 def spread_tiles(tile_set, columns, tile_count):
@@ -43,7 +56,7 @@
     extent = p_tiles.shape[2]
     tile_count = lax.axis_size("row")
     expanded = spread_tiles(p_tiles, p_cols, tile_count)
-    transposed = lax.all_to_all(expanded, "row", split_axis=0, concat_axis=1, tiled=True)
+    transposed = _apply_task(expanded, 0, 1)
     empty = jnp.zeros((transposed.shape[0], tile_count * extent), jnp.float32)
     partial_sum = fold_tiles(
         empty,

time: 608 us -> 575 us (0.946)
  waiting for transfers between devices: 130 us -> 75.6 us
  local copies, waits for them, and re-layouts: 141 us -> 173 us
  blocking collectives: 155 us -> 144 us
    all_gather x1, waiting for transfers between devices: 77.6 us -> 22.1 us  [body(): lax.all_gather(q_tiles, 'row', axis=0, tiled=True)]
    unnamed x2 -> x45, local copies, waits for them, and re-layouts: 0.01 us -> 24.2 us
    split x0 -> x34, local copies, waits for them, and re-layouts: none -> 14.1 us  [_apply_task(): jnp.split(xin, lax.axis_size('row'), axis=in_dim)]
    all_gather x1, blocking collectives: 155 us -> 144 us  [body(): lax.all_gather(q_cols, 'row', axis=0, tiled=True)]
    scatter x2 -> x1, local copies, waits for them, and re-layouts: 8.73 us -> 2.27 us  [spread_tiles(): placed = placed.at[columns, :, fine_ids, :].set(flipped)]
  transfers between devices with their start and end apart: 3 -> 3, of which waited for: 2 -> 2; matrix products, arithmetic and copies ran while one was open for 2% -> 8% of each run, Pallas kernels for 0% -> 0%
where the time goes in v1:
time: 575 us; the launch traced here: 571 us
  local copies, waits for them, and re-layouts  173 us (30%)
  blocking collectives  144 us (25%)
  other arithmetic  109 us (19%)
  waiting for transfers between devices  75.6 us (13%)
  matrix products  32.9 us (6%)
  between operations  13.6 us (2%)
  starting transfers between devices  12.8 us (2%)
  loops' own time  10.7 us (2%)
    all_gather x1, blocking collectives, body(): lax.all_gather(q_cols, 'row', axis=0, tiled=True)  144 us
    scatter-add x16, other arithmetic, one_group(): tiled.at[:, coarse_ids, :]  108 us
    reduce_scatter x1, waiting for transfers between devices, body(): return lax.psum_scatter(partial_sum, 'col', scatter_dimension=1, tiled=True)  52.7 us
    reshape x16, local copies, waits for them, and re-layouts, one_group(): product.reshape(height, bundle * per_block, extent)  37.3 us
    dot_general x16, matrix products, one_group(): jnp.einsum('rfa,fkab->rfkb', stripe, bundle_tiles, preferred_element_type...  32.9 us
    reshape x16, local copies, waits for them, and re-layouts, one_group(): tiled = running.reshape(height, -1, extent)  30.7 us
    scatter-add x16, local copies, waits for them, and re-layouts, one_group(): tiled.at[:, coarse_ids, :]  29.5 us
    unnamed x45, local copies, waits for them, and re-layouts  24.2 us
  transfers between devices with their start and end apart: 3, of which 2 were waited for; matrix products, arithmetic and copies ran while one was open for 8% of the time, Pallas kernels for 0%

profile of v1, /device:TPU:1, one launch (start us, length us, event | category | flops | bytes accessed | tf_op | source)
XLA Modules:
  0.0 570.8 jit_solution(5482384697163614812)
XLA Ops:
  9.3 3.0 broadcast_in_dim.18
  12.3 2.3 scatter_fusion.1
  53.7 12.8 %all-to-all-start = ((bf16[32,128,512]{1,2,0:T(8,128)(2,1)}), bf16[32,128,512]{1,2,0:T(8,128)(2,1)}, u32[]{:S(2)}, u32[]{:S(2)}) async-start(bf16[32,128,512]{1,2,0:T(8,128)(2,1)} %constant_dynamic-update-slice_fusion), calls=%async_computation | async-start | bytes 8388608 | tf_op jit(solution)/shard_map/all_to_all | solution.py:10
  66.5 143.8 %all-gather = s32[32,4,6]{2,1,0:T(4,128)S(1)} all-gather(s32[1,4,6]{2,1,0:T(4,128)S(1)} %bitcast.130), channel_id=1, replica_groups=mesh['row'=32,'col'=8] {'row'}, dimensions={0}, use_global_device_ids=true | all-gather | bytes 3168 | tf_op jit(solution)/shard_map/all_gather | solution.py:65
  210.4 22.1 %all-gather.3.cloned.1.call-done = bf16[128,6,128,128]{3,2,1,0:T(8,128)(2,1)} async-done(((bf16[4,6,128,128]{3,2,1,0:T(8,128)(2,1)}), bf16[128,6,128,128]{3,2,1,0:T(8,128)(2,1)}) %all-gather.3.cloned.1.call-update) | async-done | bytes 25165840 | tf_op jit(solution)/shard_map/all_gather | solution.py:64
  234.0 274.3 %while.12 = (s32[]{:T(128)}, f32[128,4096]{0,1:T(8,128)}, s32[16,48]{1,0:T(8,128)S(1)}, bf16[16,8,6,128,128]{4,3,2,1,0:T(8,128)(2,1)}, s32[16]{0:T(128)S(1)}, /*...) while((s32[]{:T(128)}, f32[128,4096]{0,1:T(8,128)}, ...), condition=%wide.region_3.4_spmd, body=%wide.region_1.3_spmd.sunk | while | flops 202113168 | bytes 29623528 | solution.py:51
  236.2 2.1 fusion.19
  238.3 2.3 copy.97
  242.6 6.7 %scatter_fusion = f32[128,32,128]{2,0,1:T(8,128)S(1)} fusion(f32[128,32,128]{2,0,1:T(8,128)S(1)} %copy.96, s32[48]{0:T(128)S(1)} %fusion.18, f32[48,128,128]{2,1,0:T(8,128)} %bitcast.92), kind=kCustom, calls=%fused_computation.clone.1 | custom fusion | flops 786432 | bytes 9437376 | tf_op jit(solution)/shard_map/while/body/eval_jaxpr/scatter-add | solution.py:47
  253.4 2.1 fusion.19
  255.5 2.3 copy.97
  259.7 6.7 %scatter_fusion = f32[128,32,128]{2,0,1:T(8,128)S(1)} fusion(f32[128,32,128]{2,0,1:T(8,128)S(1)} %copy.96, s32[48]{0:T(128)S(1)} %fusion.18, f32[48,128,128]{2,1,0:T(8,128)} %bitcast.92), kind=kCustom, calls=%fused_computation.clone.1 | custom fusion | flops 786432 | bytes 9437376 | tf_op jit(solution)/shard_map/while/body/eval_jaxpr/scatter-add | solution.py:47
  270.5 2.1 fusion.19
  272.6 2.3 copy.97
  276.9 6.7 %scatter_fusion = f32[128,32,128]{2,0,1:T(8,128)S(1)} fusion(f32[128,32,128]{2,0,1:T(8,128)S(1)} %copy.96, s32[48]{0:T(128)S(1)} %fusion.18, f32[48,128,128]{2,1,0:T(8,128)} %bitcast.92), kind=kCustom, calls=%fused_computation.clone.1 | custom fusion | flops 786432 | bytes 9437376 | tf_op jit(solution)/shard_map/while/body/eval_jaxpr/scatter-add | solution.py:47
  289.7 2.3 copy.97
  294.0 6.7 %scatter_fusion = f32[128,32,128]{2,0,1:T(8,128)S(1)} fusion(f32[128,32,128]{2,0,1:T(8,128)S(1)} %copy.96, s32[48]{0:T(128)S(1)} %fusion.18, f32[48,128,128]{2,1,0:T(8,128)} %bitcast.92), kind=kCustom, calls=%fused_computation.clone.1 | custom fusion | flops 786432 | bytes 9437376 | tf_op jit(solution)/shard_map/while/body/eval_jaxpr/scatter-add | solution.py:47
  306.9 2.3 copy.97
  311.1 6.7 %scatter_fusion = f32[128,32,128]{2,0,1:T(8,128)S(1)} fusion(f32[128,32,128]{2,0,1:T(8,128)S(1)} %copy.96, s32[48]{0:T(128)S(1)} %fusion.18, f32[48,128,128]{2,1,0:T(8,128)} %bitcast.92), kind=kCustom, calls=%fused_computation.clone.1 | custom fusion | flops 786432 | bytes 9437376 | tf_op jit(solution)/shard_map/while/body/eval_jaxpr/scatter-add | solution.py:47
  322.0 2.1 fusion.19
  324.0 2.3 copy.97
  328.3 6.7 %scatter_fusion = f32[128,32,128]{2,0,1:T(8,128)S(1)} fusion(f32[128,32,128]{2,0,1:T(8,128)S(1)} %copy.96, s32[48]{0:T(128)S(1)} %fusion.18, f32[48,128,128]{2,1,0:T(8,128)} %bitcast.92), kind=kCustom, calls=%fused_computation.clone.1 | custom fusion | flops 786432 | bytes 9437376 | tf_op jit(solution)/shard_map/while/body/eval_jaxpr/scatter-add | solution.py:47
  341.2 2.3 copy.97
  345.4 6.7 %scatter_fusion = f32[128,32,128]{2,0,1:T(8,128)S(1)} fusion(f32[128,32,128]{2,0,1:T(8,128)S(1)} %copy.96, s32[48]{0:T(128)S(1)} %fusion.18, f32[48,128,128]{2,1,0:T(8,128)} %bitcast.92), kind=kCustom, calls=%fused_computation.clone.1 | custom fusion | flops 786432 | bytes 9437376 | tf_op jit(solution)/shard_map/while/body/eval_jaxpr/scatter-add | solution.py:47
  358.3 2.3 copy.97
  362.6 6.7 %scatter_fusion = f32[128,32,128]{2,0,1:T(8,128)S(1)} fusion(f32[128,32,128]{2,0,1:T(8,128)S(1)} %copy.96, s32[48]{0:T(128)S(1)} %fusion.18, f32[48,128,128]{2,1,0:T(8,128)} %bitcast.92), kind=kCustom, calls=%fused_computation.clone.1 | custom fusion | flops 786432 | bytes 9437376 | tf_op jit(solution)/shard_map/while/body/eval_jaxpr/scatter-add | solution.py:47
  375.5 2.3 copy.97
  379.7 6.7 %scatter_fusion = f32[128,32,128]{2,0,1:T(8,128)S(1)} fusion(f32[128,32,128]{2,0,1:T(8,128)S(1)} %copy.96, s32[48]{0:T(128)S(1)} %fusion.18, f32[48,128,128]{2,1,0:T(8,128)} %bitcast.92), kind=kCustom, calls=%fused_computation.clone.1 | custom fusion | flops 786432 | bytes 9437376 | tf_op jit(solution)/shard_map/while/body/eval_jaxpr/scatter-add | solution.py:47
  390.5 2.1 fusion.19
  392.6 2.3 copy.97
  396.9 6.7 %scatter_fusion = f32[128,32,128]{2,0,1:T(8,128)S(1)} fusion(f32[128,32,128]{2,0,1:T(8,128)S(1)} %copy.96, s32[48]{0:T(128)S(1)} %fusion.18, f32[48,128,128]{2,1,0:T(8,128)} %bitcast.92), kind=kCustom, calls=%fused_computation.clone.1 | custom fusion | flops 786432 | bytes 9437376 | tf_op jit(solution)/shard_map/while/body/eval_jaxpr/scatter-add | solution.py:47
  407.7 2.1 fusion.19
  409.7 2.3 copy.97
  414.0 6.7 %scatter_fusion = f32[128,32,128]{2,0,1:T(8,128)S(1)} fusion(f32[128,32,128]{2,0,1:T(8,128)S(1)} %copy.96, s32[48]{0:T(128)S(1)} %fusion.18, f32[48,128,128]{2,1,0:T(8,128)} %bitcast.92), kind=kCustom, calls=%fused_computation.clone.1 | custom fusion | flops 786432 | bytes 9437376 | tf_op jit(solution)/shard_map/while/body/eval_jaxpr/scatter-add | solution.py:47
  426.9 2.3 copy.97
  431.1 6.7 %scatter_fusion = f32[128,32,128]{2,0,1:T(8,128)S(1)} fusion(f32[128,32,128]{2,0,1:T(8,128)S(1)} %copy.96, s32[48]{0:T(128)S(1)} %fusion.18, f32[48,128,128]{2,1,0:T(8,128)} %bitcast.92), kind=kCustom, calls=%fused_computation.clone.1 | custom fusion | flops 786432 | bytes 9437376 | tf_op jit(solution)/shard_map/while/body/eval_jaxpr/scatter-add | solution.py:47
  444.0 2.3 copy.97
  448.3 6.7 %scatter_fusion = f32[128,32,128]{2,0,1:T(8,128)S(1)} fusion(f32[128,32,128]{2,0,1:T(8,128)S(1)} %copy.96, s32[48]{0:T(128)S(1)} %fusion.18, f32[48,128,128]{2,1,0:T(8,128)} %bitcast.92), kind=kCustom, calls=%fused_computation.clone.1 | custom fusion | flops 786432 | bytes 9437376 | tf_op jit(solution)/shard_map/while/body/eval_jaxpr/scatter-add | solution.py:47
  459.1 2.1 fusion.19
  461.2 2.3 copy.97
  465.4 6.7 %scatter_fusion = f32[128,32,128]{2,0,1:T(8,128)S(1)} fusion(f32[128,32,128]{2,0,1:T(8,128)S(1)} %copy.96, s32[48]{0:T(128)S(1)} %fusion.18, f32[48,128,128]{2,1,0:T(8,128)} %bitcast.92), kind=kCustom, calls=%fused_computation.clone.1 | custom fusion | flops 786432 | bytes 9437376 | tf_op jit(solution)/shard_map/while/body/eval_jaxpr/scatter-add | solution.py:47
  478.3 2.3 copy.97
  482.6 6.7 %scatter_fusion = f32[128,32,128]{2,0,1:T(8,128)S(1)} fusion(f32[128,32,128]{2,0,1:T(8,128)S(1)} %copy.96, s32[48]{0:T(128)S(1)} %fusion.18, f32[48,128,128]{2,1,0:T(8,128)} %bitcast.92), kind=kCustom, calls=%fused_computation.clone.1 | custom fusion | flops 786432 | bytes 9437376 | tf_op jit(solution)/shard_map/while/body/eval_jaxpr/scatter-add | solution.py:47
  493.4 2.1 fusion.19
  495.5 2.3 copy.97
  499.7 6.7 %scatter_fusion = f32[128,32,128]{2,0,1:T(8,128)S(1)} fusion(f32[128,32,128]{2,0,1:T(8,128)S(1)} %copy.96, s32[48]{0:T(128)S(1)} %fusion.18, f32[48,128,128]{2,1,0:T(8,128)} %bitcast.92), kind=kCustom, calls=%fused_computation.clone.1 | custom fusion | flops 786432 | bytes 9437376 | tf_op jit(solution)/shard_map/while/body/eval_jaxpr/scatter-add | solution.py:47
  508.3 2.9 copy.88
  511.2 52.7 %reduce-scatter.2.cloned.1.call-done = f32[128,512]{1,0:T(8,128)} async-done(((f32[128,4096]{1,0:T(8,128)}), f32[128,512]{1,0:T(8,128)}) %reduce-scatter.2.cloned.1.call-update) | async-done | bytes 262160 | tf_op jit(solution)/shard_map/reduce_scatter | solution.py:67
  (180 shorter events, 145.3 us)
Async XLA Ops:
  6.5 226.0 %all-gather.3.cloned.1.call-start = ((), (), s32[]{:S(2)}) async-start(), calls=%async_computation.2 | async-start | bytes 25952256 | tf_op jit(solution)/shard_map/all_gather | solution.py:64
  23.7 8.7 %copy-start = (bf16[1,128,4,128]{1,3,2,0:T(8,128)(2,1)S(1)}, bf16[1,128,4,128]{1,3,2,0:T(8,128)(2,1)}, u32[]{:S(2)}) copy-start(bf16[1,128,4,128]{1,3,2,0:T(8,128)(2,1)} %copy.59) | copy-start | bytes 393220
  24.5 7.2 %copy-start.1 = (bf16[1,128,4,128]{1,3,2,0:T(8,128)(2,1)S(1)}, bf16[1,128,4,128]{1,3,2,0:T(8,128)(2,1)}, u32[]{:S(2)}) copy-start(bf16[1,128,4,128]{1,3,2,0:T(8,128)(2,1)} %copy.58) | copy-start | bytes 393220
  25.3 5.8 %copy-start.2 = (bf16[1,128,4,128]{1,3,2,0:T(8,128)(2,1)S(1)}, bf16[1,128,4,128]{1,3,2,0:T(8,128)(2,1)}, u32[]{:S(2)}) copy-start(bf16[1,128,4,128]{1,3,2,0:T(8,128)(2,1)} %copy.57) | copy-start | bytes 393220
  26.1 4.4 copy-start.3
  28.8 14.3 %copy-start.5 = (bf16[1,128,4,128]{1,3,2,0:T(8,128)(2,1)S(1)}, bf16[1,128,4,128]{1,3,2,0:T(8,128)(2,1)}, u32[]{:S(2)}) copy-start(bf16[1,128,4,128]{1,3,2,0:T(8,128)(2,1)} %copy.71) | copy-start | bytes 393220
  28.8 15.0 %copy-start.4 = (bf16[1,128,4,128]{1,3,2,0:T(8,128)(2,1)S(1)}, bf16[1,128,4,128]{1,3,2,0:T(8,128)(2,1)}, u32[]{:S(2)}) copy-start(bf16[1,128,4,128]{1,3,2,0:T(8,128)(2,1)} %copy.72) | copy-start | bytes 393220
  53.7 12.8 %copy-start.6 = (s32[4,6]{1,0:T(4,128)S(1)}, s32[4,6]{1,0:T(4,128)}, u32[]{:S(2)}) copy-start(s32[4,6]{1,0:T(4,128)} %param.9) | copy-start | bytes 292
  53.7 156.7 %all-to-all-start = ((bf16[32,128,512]{1,2,0:T(8,128)(2,1)}), bf16[32,128,512]{1,2,0:T(8,128)(2,1)}, u32[]{:S(2)}, u32[]{:S(2)}) async-start(bf16[32,128,512]{1,2,0:T(8,128)(2,1)} %constant_dynamic-update-slice_fusion), calls=%async_computation | async-start | bytes 8388608 | tf_op jit(solution)/shard_map/all_to_all | solution.py:10
  66.5 497.5 %reduce-scatter.2.cloned.1.call-start = ((), (), s32[]{:S(2)}) async-start(), calls=%async_computation.3 | async-start | bytes 2359296 | tf_op jit(solution)/shard_map/reduce_scatter | solution.py:67
Sparse Core Ops, SparseCore 0:
  10.1 222.3 all-gather.2
  511.3 52.5 reduce-scatter.1
